TPU v7x, 128 devices: a whole 4x4x4 slice. The times are simulated.
128 devices in a mesh: site: 4 (over z), blk: 16 (over x, y), charge: 2 (over core).
Axes of the slice: x: 4, y: 4, z: 4, core: 2. Of those that a mesh axis runs over, the one named last changes fastest.
Arguments:
- theta: bfloat16 [4, 64, 128, 2048], P('site', ('blk', 'charge')), may hold values from -6 to 6
- boundary_env: bfloat16 [64, 18, 128, 128], P(('blk', 'charge')), may hold values from -1 to 1
- right_env: bfloat16 [4, 64, 18, 128, 128], P('site', ('blk', 'charge')), may hold values from -1 to 1
- site_tensors: bfloat16 [4, 2, 64, 4, 128, 128], P('site', None, ('blk', 'charge')), may hold values from -0.375 to 0.375
- site_mpo: bfloat16 [4, 2, 18, 18, 4, 4], P('site'), may hold values from -0.75 to 0.75
- bond_ops: bfloat16 [4, 18, 16, 16], P('site'), may hold values from -1 to 1
- block_energy: float32 [4, 64], P('site', ('blk', 'charge')), may hold values from 1 to 4
- sector_charge: int32 [4, 64], P('site', ('blk', 'charge')), may hold values from 0 to 63, as said below
- block_len: int32 [4, 64], P('site', ('blk', 'charge')), may hold values from 64 to 128
- channel_charge: int32 [18], replicated, may hold values from -1 to 1
Outputs:
- env_out: bfloat16 [4, 64, 18, 128, 128], P('site', ('blk', 'charge'))
- lanczos: bfloat16 [4, 64, 128, 2048], P('site', ('blk', 'charge'))
- coefficients: float32 [4, 2], P('site')
Inputs may be any that keep to these rules, and one draw needn't show every extreme that they name: `sector_charge`: in each section every label of 0 to 63 appears exactly once; the blocks held at index c of the charge axis carry labels of parity c.
All inputs are finite; a program needn't handle non-finite values.
Results may differ from a plain program's by a relative error of at most 0.03.
Values may be sent and summed in bfloat16 or wider, within the bound.
A program may use at most 128 MiB of HBM per device.

v0:
```python
import jax
import jax.numpy as jnp
from jax import lax
from jax.sharding import PartitionSpec as P

BS = 128
M = 2048
NS = 64


def from_behind(block, axis, distance):
    devices = range(lax.axis_size(axis))
    route = [(i - distance, i) for i in devices if i - distance in devices]
    return lax.ppermute(block, axis, route)


def from_partner(shard, axis, bit):
    return lax.ppermute(shard, axis, [(i, i ^ 1 << bit) for i in range(lax.axis_size(axis))])


def env_update(environ, tensors, site_op):

    def one_block(entries):
        env_block, site_blocks = entries
        left_part = jnp.einsum(
            "wab,sbc->wsac", env_block, site_blocks, preferred_element_type=jnp.float32
        ).astype(jnp.bfloat16)
        mixed = jnp.einsum(
            "wvts,wsac->vtac", site_op, left_part, preferred_element_type=jnp.float32
        ).astype(jnp.bfloat16)
        return jnp.einsum(
            "tab,vtac->vbc", site_blocks, mixed, preferred_element_type=jnp.float32
        ).astype(jnp.bfloat16)

    return lax.map(one_block, (environ, tensors))


def block_product(env_block, right_blocks, chosen, ops, charges):

    def segment(total_sum, entries):
        left_block, right_block, bond_op, charge = entries
        source_tile = lax.dynamic_index_in_dim(chosen, charge + 1, 0, keepdims=False)
        contracted = jnp.dot(left_block, source_tile, preferred_element_type=jnp.float32).astype(
            jnp.bfloat16
        )
        shaped = contracted.reshape(contracted.shape[0], ops.shape[1], -1)
        applied = jnp.einsum(
            "asb,bc->asc", shaped, right_block, preferred_element_type=jnp.float32
        ).astype(jnp.bfloat16)
        final = jnp.einsum("asc,st->atc", applied, bond_op, preferred_element_type=jnp.float32)
        return (total_sum + final.reshape(total_sum.shape), None)

    start_sum = jnp.zeros((chosen.shape[1], chosen.shape[2]), jnp.float32)
    return lax.scan(segment, start_sum, (env_block, right_blocks, ops, charges))[0]


def keep_same(values):
    return values


def pair_with(environ, tensors, site_ops):
    first = env_update(environ, tensors[0], site_ops[0])
    return env_update(first, tensors[1], site_ops[1])


def picker(wanted_labels, pieces):
    sign_pair = jnp.array([-1, 1], jnp.int32)
    wanted = wanted_labels[:, None] + sign_pair[None, :]
    incoming_tiles, incoming_tags = pieces
    matches = (incoming_tags[None, None, :] == wanted[:, :, None]).astype(jnp.bfloat16)
    picked = jnp.einsum(
        "kst,tam->ksam", matches, incoming_tiles, preferred_element_type=jnp.float32
    )
    return picked.astype(jnp.bfloat16)


def on_device(
    theta,
    boundary_env,
    right_env,
    site_tensors,
    site_mpo,
    bond_ops,
    block_energy,
    sector_charge,
    block_len,
    channel_charge,
):
    section = lax.axis_index("site")
    site_count = lax.axis_size("site")
    tensors = site_tensors[0]
    site_ops = site_mpo[0]

    def update_pair(environ):
        return pair_with(environ, tensors, site_ops)

    state = boundary_env
    env_in = boundary_env
    for segment in range(site_count):
        state = lax.cond(section == segment, update_pair, keep_same, state)
        if segment + 1 < site_count:
            received = from_behind(state, "site", 1)
            is_next = section == segment + 1
            state = jnp.where(is_next, received, state)
            env_in = jnp.where(is_next, received, env_in)
    labels = sector_charge[0]
    live_rows = block_len[0]
    row_mask = jnp.arange(theta.shape[2], dtype=jnp.int32)[None, :] < live_rows[:, None]
    theta_m = theta[0] * row_mask[:, :, None].astype(jnp.bfloat16)
    other_labels = from_partner(labels, "charge", 0)
    for_other = picker(
        other_labels,
        (
            lax.all_gather(theta_m, "blk", axis=0, tiled=True),
            lax.all_gather(labels, "blk", axis=0, tiled=True),
        ),
    )
    partner = from_partner(for_other, "charge", 0)
    chosen_all = jnp.stack([partner[:, 0], theta_m, partner[:, 1]], axis=1)
    ops = bond_ops[0]

    def per_block(entries):
        return block_product(entries[0], entries[1], entries[2], ops, channel_charge)

    product = lax.map(per_block, (env_in, right_env[0], chosen_all))
    theta_f = theta_m.astype(jnp.float32)
    product = (
        product * row_mask[:, :, None].astype(jnp.float32)
        - block_energy[0][:, None, None] * theta_f
    )
    entries_count = NS * BS * M
    correlation, norm_theta = lax.psum(
        (jnp.sum(theta_f * product), jnp.sum(theta_f * theta_f)), ("blk", "charge")
    )
    rayleigh = correlation / norm_theta
    residual = product - rayleigh * theta_f
    residual_sq = lax.psum(jnp.sum(residual * residual), ("blk", "charge"))
    mean_sq = residual_sq / entries_count
    lanczos = (residual / jnp.sqrt(mean_sq + 1e-06)).astype(jnp.bfloat16)
    coefficients = jnp.stack([rayleigh, jnp.sqrt(mean_sq)])[None, :]
    return (state[None], lanczos[None], coefficients)


def solution(mesh):
    return jax.shard_map(
        on_device,
        mesh=mesh,
        in_specs=(
            P("site", ("blk", "charge"), None, None),
            P(("blk", "charge"), None, None, None),
            P("site", ("blk", "charge"), None, None, None),
            P("site", None, ("blk", "charge"), None, None, None),
            P("site", None, None, None, None, None),
            P("site", None, None, None),
            P("site", ("blk", "charge")),
            P("site", ("blk", "charge")),
            P("site", ("blk", "charge")),
            P(),
        ),
        out_specs=(
            P("site", ("blk", "charge"), None, None, None),
            P("site", ("blk", "charge"), None, None),
            P("site", None),
        ),
        check_vma=False,
    )
```

profile of v0, /device:TPU:97, one launch (start us, length us, event | category | flops | bytes accessed | tf_op | source)
XLA Modules:
  0.0 685.1 jit_solution(11959686821084895500)
XLA Ops:
  9.1 2.4 bitcast_multiply_fusion
  18.5 13.5 %all-reduce = s32[32]{0:T(128)S(1)} all-reduce(s32[32]{0:T(128)S(1)} %bitcast_dynamic-update-slice_fusion.1), channel_id=2, replica_groups=mesh['site'=4,'blk'=16,'charge'=2] {'blk'}, use_global_device_ids=true, to_apply=%add | all-reduce | flops 32 | bytes 256
  32.1 11.6 %collective-permute-done = bf16[2,18,128,128]{3,2,1,0:T(8,128)(2,1)S(1)} collective-permute-done((bf16[2,18,128,128]{3,2,1,0:T(8,128)(2,1)}, bf16[2,18,128,128]{3,2,1,0:T(8,128)(2,1)S(1)}, u32[]{:S(2)}, u32[]{:S(2)}) %collective-permute-start) | collective-permute-done | bytes 1179680 | tf_op jit(solution)/shard_map/ppermute | solution.py:14
  43.7 1.8 broadcast_select_fusion
  45.6 1.5 collective-permute-start.1
  47.0 77.2 %all-gather.3.cloned.1.call-done = bf16[32,128,2048]{2,1,0:T(8,128)(2,1)} async-done(((bf16[2,128,2048]{2,1,0:T(8,128)(2,1)}), bf16[32,128,2048]{2,1,0:T(8,128)(2,1)}) %all-gather.3.cloned.1.call-update) | async-done | bytes 16777232 | tf_op jit(solution)/shard_map/all_gather | solution.py:114
  124.2 26.1 %fusion.233 = bf16[2,2,128,2048]{3,1,2,0:T(2,128)(2,1)} fusion(bf16[32,128,2048]{2,1,0:T(8,128)(2,1)} %all-gather.3.cloned.1.call-done, s32[32]{0:T(128)S(1)} %all-reduce, s32[2,2]{1,0:T(2,128)S(1)} %broadcast_add_fusion), kind=kOutput, calls=%fused_computation.203 | convolution fusion | flops 68157568 | bytes 18874512 | tf_op jit(solution)/shard_map/kst,tam->ksam/dot_general | solution.py:71
  151.6 9.2 %collective-permute-start.2 = (bf16[2,18,128,128]{3,2,1,0:T(8,128)(2,1)S(1)}, bf16[2,18,128,128]{3,2,1,0:T(8,128)(2,1)}, u32[]{:S(2)}, u32[]{:S(2)}) collective-permute-start(bf16[2,18,128,128]{3,2,1,0:T(8,128)(2,1)S(1)} %get-tuple-element.589), channel_id=1, source_target_pairs={{0,32},{32,64},{64,96},{1,33},{33,65},{65,97},{2,34},{34,66},{66,9... | collective-permute-start | bytes 3538952 | tf_op jit(solution)/shard_map/ppermute | solution.py:14
  160.8 1.7 copy.99
  162.5 2.2 copy_multiply_fusion
  164.7 85.6 %collective-permute-done.2 = bf16[2,18,128,128]{3,2,1,0:T(8,128)(2,1)} collective-permute-done((bf16[2,18,128,128]{3,2,1,0:T(8,128)(2,1)S(1)}, bf16[2,18,128,128]{3,2,1,0:T(8,128)(2,1)}, u32[]{:S(2)}, u32[]{:S(2)}) %collective-permute-start.2) | collective-permute-done | bytes 1179680 | tf_op jit(solution)/shard_map/ppermute | solution.py:14
  250.4 2.7 select_select_fusion
  253.1 5.6 fusion.247
  258.6 7.1 %pad_maximum_fusion = bf16[2,3,128,2048]{3,1,2,0:T(4,128)(2,1)S(1)} fusion(bf16[2,1,128,2048]{3,1,2,0:T(2,128)(2,1)S(1)} %get-tuple-element.724, bf16[2,1,128,2048]{3,1,2,0:T(2,128)(2,1)S(1)} %copy_multiply_fusion, bf16[2,1,128,2048]{3,1,2,0:T(2,128)(2,1)S(1)} %get-tuple-element.723), kind=kLoop, calls=%fused_computation.198 | loop fusion | flops 9437184 | bytes 6291456 | tf_op jit(solution)/shard_map/stack | solution.py:119
  265.8 3.9 copy.100
  269.7 211.9 %while.113 = (s32[]{:T(128)}, f32[2,128,2048]{2,1,0:T(8,128)}, bf16[2,18,128,128]{3,2,1,0:T(8,128)(2,1)S(1)}, bf16[2,18,128,128]{3,2,1,0:T(8,128)(2,1)}, bf16[2,...) while((s32[]{:T(128)}, f32[2,128,2048]{2,1,0:T(8,128)}, ...), condition=%wide.region_27.28_spmd, body=%wide.region_24.27_spmd.sunk | while | flops 143654912 | bytes 23926256 | solution.py:125
  269.7 2.4 dynamic-slice_bitcast_fusion.5
  272.1 2.7 dynamic-slice_bitcast_fusion.6
  274.8 99.1 %while.114 = (s32[]{:T(128)}, f32[128,2048]{1,0:T(8,128)S(1)}, bf16[18,16,16]{1,2,0:T(8,128)(2,1)}, bf16[18,128,128]{2,1,0:T(8,128)(2,1)}, s32[18]{0:T(128)S(1)}...) while((s32[]{:T(128)}, f32[128,2048]{1,0:T(8,128)S(1)}, ...), condition=%wide.region_26.26_spmd.clone, body=%wide.region_25.25_spmd.clone.sunk | while | flops 143654912 | bytes 6886593 | solution.py:54
  276.9 1.4 fusion.325
  282.4 1.4 fusion.325
  287.9 1.4 fusion.325
  293.4 1.4 fusion.325
  298.9 1.4 fusion.325
  320.9 1.4 fusion.325
  343.0 1.4 fusion.325
  348.5 1.4 fusion.325
  370.5 1.4 fusion.325
  375.6 2.4 dynamic-slice_bitcast_fusion.5
  378.0 2.7 dynamic-slice_bitcast_fusion.6
  380.7 99.1 %while.114 = (s32[]{:T(128)}, f32[128,2048]{1,0:T(8,128)S(1)}, bf16[18,16,16]{1,2,0:T(8,128)(2,1)}, bf16[18,128,128]{2,1,0:T(8,128)(2,1)}, s32[18]{0:T(128)S(1)}...) while((s32[]{:T(128)}, f32[128,2048]{1,0:T(8,128)S(1)}, ...), condition=%wide.region_26.26_spmd.clone, body=%wide.region_25.25_spmd.clone.sunk | while | flops 143654912 | bytes 6886593 | solution.py:54
  382.8 1.4 fusion.325
  399.3 1.4 fusion.325
  404.8 1.4 fusion.325
  410.3 1.4 fusion.325
  415.8 1.4 fusion.325
  432.4 1.4 fusion.325
  437.9 1.4 fusion.325
  443.4 1.4 fusion.325
  448.9 1.4 fusion.325
  476.4 1.4 fusion.325
  481.5 3.8 fusion.238
  485.3 68.7 %all-reduce.1 = (f32[]{:T(128)}, f32[]{:T(128)}) all-reduce(f32[]{:T(128)} %get-tuple-element.594, f32[]{:T(128)} %get-tuple-element.593), channel_id=1, replica_groups=mesh['site'=4,'blk'=16,'charge'=2] {'blk','charge'}, use_global_device_ids=true, to_apply=%region_29.30 | all-reduce | flops 2 | bytes 16 | tf_op jit(solution)/shard_map/psum | solution.py:132
  555.4 3.3 multiply_reduce_fusion
  558.7 48.6 %conditional.7 = (bf16[1,2,18,128,128]{4,3,2,1,0:T(8,128)(2,1)}) conditional(s32[]{:T(128)} %convert_element_type.194, (bf16[2,18,128,128]{3,2,1,0:T(8,128)(2,1)S(1)}) %tuple.289, (bf16[2,2,4,128,128]{3,4,2,1,0:T(8,128)(2,1)}, bf16[2,18,18,4,4]{1,2,4,3,0:T(8,128)(2,1)}, bf16[2,18,128,128]{3,2,1,0:T(8,128)(2,1)S(1)}) %tuple.290), branch_computations={%region_18.19_spmd, %region_19.24_spmd} | conditional | flops 1553006592 | bytes 31303274 | solution.py:100
  558.7 1.9 slice_bitcast_fusion.12
  560.6 1.6 slice_bitcast_fusion.14
  562.5 21.7 %while.109 = (s32[]{:T(128)}, bf16[2,18,128,128]{2,3,1,0:T(8,128)(2,1)S(1)}, bf16[2,4,128,128]{2,3,1,0:T(8,128)(2,1)}, bf16[2,18,128,128]{3,2,1,0:T(8,128)(2,1)S(1)}, bf16[18,18,4,4]{0,1,3,2:T(8,128)(2,1)}, /*index=5*/s32[]{:T(128)}) while((s32[]{:T(128)}, bf16[2,18,128,128]{2,3,1,0:T(8,128)(2,1)S(1)}, bf16[2,4,128,128]{2,3,1,0:T(8,128)(2,1)}, ...), condition=%wide.region_21.21_spmd, body=%wide.region_20.20_spmd.sunk | while | flops 776503296 | bytes 12768005 | solution.py:35
  562.7 1.7 convert_bitcast_fusion.16
  564.4 7.2 %fusion.333 = bf16[18,4,128,128]{2,0,1,3:T(8,128)(2,1)S(1)} fusion(bf16[18,4,128,128,1]{2,3,0,1,4:T(8,128)(2,1)S(1)} %convert_bitcast_fusion.16, bf16[18,18,4,4]{0,1,3,2:T(8,128)(2,1)S(1)} %copy-done.20), kind=kOutput, calls=%fused_computation.133.clone.1 | convolution fusion | flops 171048960 | bytes 4728960 | tf_op jit(solution)/shard_map/cond/branch_1_fun/while/body/eval_jaxpr/wvts,wsac->vtac/dot_general | solution.py:28
  571.6 1.7 fusion.334
  573.4 1.7 convert_bitcast_fusion.16
  575.2 7.2 %fusion.333 = bf16[18,4,128,128]{2,0,1,3:T(8,128)(2,1)S(1)} fusion(bf16[18,4,128,128,1]{2,3,0,1,4:T(8,128)(2,1)S(1)} %convert_bitcast_fusion.16, bf16[18,18,4,4]{0,1,3,2:T(8,128)(2,1)S(1)} %copy-done.20), kind=kOutput, calls=%fused_computation.133.clone.1 | convolution fusion | flops 171048960 | bytes 4728960 | tf_op jit(solution)/shard_map/cond/branch_1_fun/while/body/eval_jaxpr/wvts,wsac->vtac/dot_general | solution.py:28
  582.4 1.7 fusion.334
  584.4 21.3 %while.110 = (s32[]{:T(128)}, bf16[2,18,128,128]{2,3,1,0:T(8,128)(2,1)S(1)}, bf16[2,4,128,128]{2,3,1,0:T(8,128)(2,1)}, bf16[2,18,128,128]{2,3,1,0:T(8,128)(2,1)S...) while((s32[]{:T(128)}, bf16[2,18,128,128]{2,3,1,0:T(8,128)(2,1)S(1)}, ...), condition=%wide.region_23.23_spmd, body=%wide.region_22.22_spmd.sunk | while | flops 776503296 | bytes 12726505 | solution.py:35
  584.4 1.7 convert_bitcast_fusion.17
  586.1 7.2 %fusion.341 = bf16[18,4,128,128]{2,0,1,3:T(8,128)(2,1)S(1)} fusion(bf16[18,4,128,128,1]{2,3,0,1,4:T(8,128)(2,1)S(1)} %convert_bitcast_fusion.17, bf16[18,18,4,4]{0,1,3,2:T(8,128)(2,1)S(1)} %get-tuple-element.1151), kind=kOutput, calls=%fused_computation.153.clone.1 | convolution fusion | flops 171048960 | bytes 4728960 | tf_op jit(solution)/shard_map/cond/branch_1_fun/while/body/eval_jaxpr/wvts,wsac->vtac/dot_general | solution.py:28
  593.3 1.7 fusion.342
  595.1 1.7 convert_bitcast_fusion.17
  596.8 7.2 %fusion.341 = bf16[18,4,128,128]{2,0,1,3:T(8,128)(2,1)S(1)} fusion(bf16[18,4,128,128,1]{2,3,0,1,4:T(8,128)(2,1)S(1)} %convert_bitcast_fusion.17, bf16[18,18,4,4]{0,1,3,2:T(8,128)(2,1)S(1)} %get-tuple-element.1151), kind=kOutput, calls=%fused_computation.153.clone.1 | convolution fusion | flops 171048960 | bytes 4728960 | tf_op jit(solution)/shard_map/cond/branch_1_fun/while/body/eval_jaxpr/wvts,wsac->vtac/dot_general | solution.py:28
  604.0 1.7 fusion.342
  605.7 1.4 copy.177
  607.4 65.9 %psum.23 = f32[]{:T(128)} all-reduce(f32[]{:T(128)} %multiply_reduce_fusion), channel_id=1, replica_groups=mesh['site'=4,'blk'=16,'charge'=2] {'blk','charge'}, use_global_device_ids=true, to_apply=%region_33.34 | all-reduce | flops 1 | bytes 8 | tf_op jit(solution)/shard_map/psum | solution.py:137
  674.0 3.3 fusion.240
  (241 shorter events, 136.4 us)
Async XLA Ops:
  7.2 4.4 copy-start.18
  7.2 5.4 copy-start.17
  7.2 117.0 %all-gather.3.cloned.1.call-start = ((), (), s32[]{:S(2)}) async-start(), calls=%async_computation | async-start | bytes 17825792 | tf_op jit(solution)/shard_map/all_gather | solution.py:114
  8.6 0.5 copy-start.21
  9.1 4.5 copy-start.2
  13.6 2.3 copy-start.26
  13.6 3.4 copy-start.28
  13.6 18.4 %copy-start.25 = (s32[2]{0:T(128)S(1)}, s32[2]{0:T(128)}, u32[]{:S(2)}) copy-start(s32[2]{0:T(128)} %constant.168.clone) | copy-start | bytes 28
  14.7 29.0 %collective-permute-start = (bf16[2,18,128,128]{3,2,1,0:T(8,128)(2,1)}, bf16[2,18,128,128]{3,2,1,0:T(8,128)(2,1)S(1)}, u32[]{:S(2)}, u32[]{:S(2)}) collective-permute-start(bf16[2,18,128,128]{3,2,1,0:T(8,128)(2,1)} %get-tuple-element.585), channel_id=1, source_target_pairs={{0,32},{32,64},{64,96},{1,33},{33,65},{65,97},{2,34},{34,66},{66,9... | collective-permute-start | bytes 3538952 | tf_op jit(solution)/shard_map/ppermute | solution.py:14
  16.0 16.0 %collective-permute-start.3 = (s32[2]{0:T(128)S(1)}, s32[2]{0:T(128)S(1)}, u32[]{:S(2)}, u32[]{:S(2)}) collective-permute-start(s32[2]{0:T(128)S(1)} %bitcast.620), channel_id=1, source_target_pairs={{0,1},{1,0},{2,3},{3,2},{4,5},{5,4},{6,7},{7,6},{8,9},{9,8},{10,11... | collective-permute-start | bytes 32 | tf_op jit(solution)/shard_map/ppermute | solution.py:18
  43.7 1.8 copy-start.8
  45.6 105.5 %collective-permute-start.1 = (bf16[2,18,128,128]{3,2,1,0:T(8,128)(2,1)S(1)}, bf16[2,18,128,128]{3,2,1,0:T(8,128)(2,1)}, u32[]{:S(2)}, u32[]{:S(2)}) collective-permute-start(bf16[2,18,128,128]{3,2,1,0:T(8,128)(2,1)S(1)} %get-tuple-element.587), channel_id=1, source_target_pairs={{0,32},{32,64},{64,96},{1,33},{33,65},{65,97},{2,34},{34,66},{66,9... | collective-permute-start | bytes 3538952 | tf_op jit(solution)/shard_map/ppermute | solution.py:14
  150.3 102.7 %collective-permute-start.4 = (bf16[2,2,128,2048]{3,1,2,0:T(2,128)(2,1)}, bf16[2,2,128,2048]{3,1,2,0:T(2,128)(2,1)}, u32[]{:S(2)}, u32[]{:S(2)}) collective-permute-start(bf16[2,2,128,2048]{3,1,2,0:T(2,128)(2,1)} %fusion.233), channel_id=1, source_target_pairs={{0,1},{1,0},{2,3},{3,2},{4,5},{5,4},{6,7},{7,6},{8,9},{9,8},{10,11... | collective-permute-start | bytes 6291464 | tf_op jit(solution)/shard_map/ppermute | solution.py:18
  151.2 11.3 %copy-start = (bf16[1,2,128,2048]{3,2,1,0:T(8,128)(2,1)S(1)}, bf16[1,2,128,2048]{3,2,1,0:T(8,128)(2,1)}, u32[]{:S(2)}) copy-start(bf16[1,2,128,2048]{3,2,1,0:T(8,128)(2,1)} %param.39) | copy-start | bytes 3145732
  151.2 11.3 %copy-start.22 = (bf16[2,128]{1,0:T(2,128)(2,1)S(1)}, bf16[2,128]{1,0:T(2,128)(2,1)}, u32[]{:S(2)}) copy-start(bf16[2,128]{1,0:T(2,128)(2,1)} %copy-done.21) | copy-start | bytes 1540
  151.6 98.7 %collective-permute-start.2 = (bf16[2,18,128,128]{3,2,1,0:T(8,128)(2,1)S(1)}, bf16[2,18,128,128]{3,2,1,0:T(8,128)(2,1)}, u32[]{:S(2)}, u32[]{:S(2)}) collective-permute-start(bf16[2,18,128,128]{3,2,1,0:T(8,128)(2,1)S(1)} %get-tuple-element.589), channel_id=1, source_target_pairs={{0,32},{32,64},{64,96},{1,33},{33,65},{65,97},{2,34},{34,66},{66,9... | collective-permute-start | bytes 3538952 | tf_op jit(solution)/shard_map/ppermute | solution.py:14
  162.5 87.9 %copy-start.9 = (bf16[2,18,128,128]{3,2,1,0:T(8,128)(2,1)S(1)}, bf16[2,18,128,128]{3,2,1,0:T(8,128)(2,1)}, u32[]{:S(2)}) copy-start(bf16[2,18,128,128]{3,2,1,0:T(8,128)(2,1)} %copy-done.8) | copy-start | bytes 3538948
  265.8 3.9 copy-start.27
  269.7 211.9 %copy-start.23 = (f32[2,128]{1,0:T(2,128)S(1)}, f32[2,128]{1,0:T(2,128)}, u32[]{:S(2)}) copy-start(f32[2,128]{1,0:T(2,128)} %get-tuple-element.727) | copy-start | bytes 3076
  269.7 211.9 %copy-start.24 = (f32[1,2]{1,0:T(1,128)S(1)}, f32[1,2]{1,0:T(1,128)}, u32[]{:S(2)}) copy-start(f32[1,2]{1,0:T(1,128)} %param.45) | copy-start | bytes 28
  269.7 5.2 copy-start.4
  374.0 1.6 copy-start.5
  375.6 5.1 copy-start.4
  479.9 1.6 copy-start.5
  481.5 73.8 %copy-start.1 = (bf16[1,2,128,2048]{3,2,1,0:T(8,128)(2,1)S(1)}, bf16[1,2,128,2048]{3,2,1,0:T(8,128)(2,1)}, u32[]{:S(2)}) copy-start(bf16[1,2,128,2048]{3,2,1,0:T(8,128)(2,1)} %param.39) | copy-start | bytes 3145732
  481.5 73.8 %copy-start.3 = (bf16[2,18,128,128]{3,2,1,0:T(8,128)(2,1)S(1)}, bf16[2,18,128,128]{3,2,1,0:T(8,128)(2,1)}, u32[]{:S(2)}) copy-start(bf16[2,18,128,128]{3,2,1,0:T(8,128)(2,1)} %get-tuple-element.726) | copy-start | bytes 3538948
  562.7 1.7 copy-start.20
  564.4 7.2 %copy-start.14 = (bf16[2,4,128,128]{2,3,1,0:T(8,128)(2,1)S(1)}, bf16[2,4,128,128]{2,3,1,0:T(8,128)(2,1)}, u32[]{:S(2)}) copy-start(bf16[2,4,128,128]{2,3,1,0:T(8,128)(2,1)} %get-tuple-element.1131) | copy-start | bytes 786436 | tf_op jit(solution)/shard_map/cond/branch_1_fun/while
  573.4 1.7 copy-start.20
  575.2 7.2 %copy-start.14 = (bf16[2,4,128,128]{2,3,1,0:T(8,128)(2,1)S(1)}, bf16[2,4,128,128]{2,3,1,0:T(8,128)(2,1)}, u32[]{:S(2)}) copy-start(bf16[2,4,128,128]{2,3,1,0:T(8,128)(2,1)} %get-tuple-element.1131) | copy-start | bytes 786436 | tf_op jit(solution)/shard_map/cond/branch_1_fun/while
  586.1 7.2 %copy-start.11 = (bf16[2,4,128,128]{2,3,1,0:T(8,128)(2,1)S(1)}, bf16[2,4,128,128]{2,3,1,0:T(8,128)(2,1)}, u32[]{:S(2)}) copy-start(bf16[2,4,128,128]{2,3,1,0:T(8,128)(2,1)} %get-tuple-element.1149) | copy-start | bytes 786436 | tf_op jit(solution)/shard_map/cond/branch_1_fun/while
  596.7 7.2 %copy-start.11 = (bf16[2,4,128,128]{2,3,1,0:T(8,128)(2,1)S(1)}, bf16[2,4,128,128]{2,3,1,0:T(8,128)(2,1)}, u32[]{:S(2)}) copy-start(bf16[2,4,128,128]{2,3,1,0:T(8,128)(2,1)} %get-tuple-element.1149) | copy-start | bytes 786436 | tf_op jit(solution)/shard_map/cond/branch_1_fun/while
Sparse Core Ops, SparseCore 0:
  11.7 112.4 all-gather.2
where the time goes:
time: 698 us; the launch traced here: 685 us
  waiting for transfers between devices  174 us (25%)
  matrix products  161 us (23%)
  blocking collectives  148 us (21%)
  local copies, waits for them, and re-layouts  62.4 us (9%)
  other arithmetic  56 us (8%)
  loops' own time  52.4 us (8%)
  between operations  17.4 us (2%)
  starting transfers between devices  13.8 us (2%)
    ppermute x3, waiting for transfers between devices, from_behind(): return lax.ppermute(block, axis, route)  97.3 us
    all_gather x1, waiting for transfers between devices, on_device(): lax.all_gather(theta_m, 'blk', axis=0, tiled=True)  77.2 us
    psum x1, blocking collectives, on_device(): lax.psum((jnp.sum(theta_f * product), jnp.sum(theta_f * theta_f)), ('blk'...  68.7 us
    psum x1, blocking collectives, on_device(): residual_sq = lax.psum(jnp.sum(residual * residual), ('blk', 'charge'))  65.9 us
    another operation x2, loops' own time, block_product(): lax.scan(segment, start_sum, (env_block, right_blocks, ops, charges))[0]  51.2 us
    dot_general x36, matrix products, segment(): jnp.dot(left_block, source_tile, preferred_element_type=jnp.float32)  48.7 us
    dot_general x36, matrix products, segment(): jnp.einsum('asc,st->atc', applied, bond_op, preferred_element_type=jnp.fl...  43.4 us
    dot_general x4, matrix products, one_block(): jnp.einsum('wvts,wsac->vtac', site_op, left_part, preferred_element_type=...  28.8 us
  transfers between devices with their start and end apart: 6, of which 3 were waited for; matrix products, arithmetic and copies ran while one was open for 6% of the time, Pallas kernels for 0%

commit v1 on v0

--- a/solution.py
+++ b/solution.py
@@ -6,6 +6,13 @@
 BS = 128
 M = 2048
 NS = 64
+
+
+def swapped_in(shard, mesh_axis, dim):
+    size = lax.axis_size(mesh_axis)
+    blocks = jnp.stack([shard for _ in range(size)])
+    blocks = lax.all_to_all(blocks, mesh_axis, split_axis=0, concat_axis=0)
+    return jnp.concatenate(blocks, axis=dim)
 
 
 def from_behind(block, axis, distance):
@@ -110,10 +117,7 @@
     other_labels = from_partner(labels, "charge", 0)
     for_other = picker(
         other_labels,
-        (
-            lax.all_gather(theta_m, "blk", axis=0, tiled=True),
-            lax.all_gather(labels, "blk", axis=0, tiled=True),
-        ),
+        (swapped_in(theta_m, "blk", 0), lax.all_gather(labels, "blk", axis=0, tiled=True)),
     )
     partner = from_partner(for_other, "charge", 0)
     chosen_all = jnp.stack([partner[:, 0], theta_m, partner[:, 1]], axis=1)

time: 698 us -> 867 us (1.24)
  blocking collectives: 148 us -> 408 us
  waiting for transfers between devices: 174 us -> 90.4 us
  local copies, waits for them, and re-layouts: 62.4 us -> 110 us
  matrix products: 161 us -> 120 us
  between operations: 17.4 us -> 3.95 us
    unnamed x1, blocking collectives: 13.5 us -> 279 us
    all_gather x1 -> x0, waiting for transfers between devices: 77.2 us -> none  [on_device(): lax.all_gather(theta_m, 'blk', axis=0, tiled=True)]
    reshape x0 -> x1, local copies, waits for them, and re-layouts: none -> 24.9 us  [swapped_in(): return jnp.concatenate(blocks, axis=dim)]
    dot_general x36, matrix products: 43.4 us -> 19.1 us  [segment(): jnp.einsum('asc,st->atc', applied, bond_op, preferred_element_type=jnp.fl...]
    dot_general x1, matrix products: 26.1 us -> 9.76 us  [picker(): jnp.einsum('kst,tam->ksam', matches, incoming_tiles, preferred_element_ty...]
    all_to_all x0 -> x1, local copies, waits for them, and re-layouts: none -> 15.4 us  [swapped_in(): blocks = lax.all_to_all(blocks, mesh_axis, split_axis=0, concat_axis=0)]
    another operation x2 -> x4, local copies, waits for them, and re-layouts: 0.52 us -> 15.9 us  [the longest x2 15.3 us: swapped_in(): blocks = jnp.stack([shard for _ in range(size)])]
  transfers between devices with their start and end apart: 6 -> 6, of which waited for: 3 -> 1; matrix products, arithmetic and copies ran while one was open for 6% -> 7% of each run, Pallas kernels for 0% -> 0%
where the time goes in v1:
time: 867 us; the launch traced here: 862 us
  blocking collectives  408 us (47%)
  matrix products  120 us (14%)
  local copies, waits for them, and re-layouts  110 us (13%)
  waiting for transfers between devices  90.4 us (10%)
  other arithmetic  59 us (7%)
  loops' own time  48.7 us (6%)
  starting transfers between devices  21.5 us (2%)
    unnamed x1, blocking collectives  279 us
    ppermute x3, waiting for transfers between devices, from_behind(): return lax.ppermute(block, axis, route)  90.4 us
    psum x1, blocking collectives, on_device(): lax.psum((jnp.sum(theta_f * product), jnp.sum(theta_f * theta_f)), ('blk'...  65.5 us
    psum x1, blocking collectives, on_device(): residual_sq = lax.psum(jnp.sum(residual * residual), ('blk', 'charge'))  63.2 us
    dot_general x36, matrix products, segment(): jnp.dot(left_block, source_tile, preferred_element_type=jnp.float32)  48.7 us
    another operation x2, loops' own time, block_product(): lax.scan(segment, start_sum, (env_block, right_blocks, ops, charges))[0]  47.5 us
    dot_general x4, matrix products, one_block(): jnp.einsum('wvts,wsac->vtac', site_op, left_part, preferred_element_type=...  28.8 us
    add x36, other arithmetic, segment(): return (total_sum + final.reshape(total_sum.shape), None)  27.1 us
  transfers between devices with their start and end apart: 6, of which 1 were waited for; matrix products, arithmetic and copies ran while one was open for 7% of the time, Pallas kernels for 0%

profile of v1, /device:TPU:97, one launch (start us, length us, event | category | flops | bytes accessed | tf_op | source)
XLA Modules:
  0.0 861.9 jit_solution(17724259683448823925)
XLA Ops:
  2.4 1.4 multiply_bitcast_fusion
  4.8 14.3 %stack.13 = bf16[16,2,128,2048]{3,1,2,0:T(2,128)(2,1)} broadcast(bf16[2,128,2048]{2,0,1:T(2,128)(2,1)S(1)} %copy.91), dimensions={1,2,3} | broadcast | bytes 17825792 | tf_op jit(solution)/shard_map/stack | solution.py:13
  19.1 6.9 all-to-all-start
  26.7 1.5 conditional.4
  29.6 8.4 collective-permute-start.3
  39.4 279.3 %all-reduce = s32[32]{0:T(128)S(1)} all-reduce(s32[32]{0:T(128)S(1)} %bitcast_dynamic-update-slice_fusion.1), channel_id=2, replica_groups=mesh['site'=4,'blk'=16,'charge'=2] {'blk'}, use_global_device_ids=true, to_apply=%add | all-reduce | flops 32 | bytes 256
  318.8 2.8 broadcast_select_fusion
  321.6 1.7 collective-permute-start.1
  323.3 15.4 %copy.92 = bf16[16,2,128,2048]{3,1,0,2:T(2,128)(2,1)} copy(bf16[16,2,128,2048]{3,1,2,0:T(2,128)(2,1)} %all-to-all-done) | data formatting | bytes 33554432 | tf_op jit(solution)/shard_map/all_to_all | solution.py:14
  338.7 24.9 %reshape.183 = bf16[32,128,2048,1]{2,0,1,3:T(8,128)(2,1)} reshape(bf16[16,2,128,2048]{3,1,0,2:T(2,128)(2,1)} %copy.92) | data formatting | bytes 33554432 | tf_op jit(solution)/shard_map/reshape | solution.py:15
  363.6 9.8 %convolution_convert_fusion.2 = bf16[2,2,128,2048]{3,1,2,0:T(2,128)(2,1)} fusion(bf16[32,128,2048,1]{2,0,1,3:T(8,128)(2,1)} %reshape.183, s32[32]{0:T(128)S(1)} %all-reduce, s32[2,2]{1,0:T(2,128)S(1)} %broadcast_add_fusion), kind=kOutput, calls=%fused_computation.200 | convolution fusion | flops 68157568 | bytes 18874512 | tf_op jit(solution)/shard_map/kst,tam->ksam/dot_general | solution.py:78
  373.4 1.6 collective-permute-start.4
  374.9 2.8 broadcast_select_fusion.1
  377.8 1.6 collective-permute-start.2
  380.5 2.2 copy_multiply_fusion
  382.7 90.4 %collective-permute-done.2 = bf16[2,18,128,128]{3,2,1,0:T(8,128)(2,1)} collective-permute-done((bf16[2,18,128,128]{3,2,1,0:T(8,128)(2,1)}, bf16[2,18,128,128]{3,2,1,0:T(8,128)(2,1)}, u32[]{:S(2)}, u32[]{:S(2)}) %collective-permute-start.2) | collective-permute-done | bytes 1179680 | tf_op jit(solution)/shard_map/ppermute | solution.py:21
  473.1 3.2 select_select_fusion
  476.3 5.6 fusion.241
  481.9 7.1 pad_maximum_fusion
  489.0 3.9 copy.95
  492.9 180.4 %while.113 = (s32[]{:T(128)}, f32[2,128,2048]{2,1,0:T(8,128)}, bf16[2,18,128,128]{3,2,1,0:T(8,128)(2,1)}, bf16[2,18,128,128]{3,2,1,0:T(8,128)(2,1)}, bf16[2,3,12...) while((s32[]{:T(128)}, f32[2,128,2048]{2,1,0:T(8,128)}, ...), condition=%wide.region_27.28_spmd, body=%wide.region_24.27_spmd.sunk | while | flops 143654912 | bytes 14490018 | solution.py:129
  492.9 2.2 dynamic-slice_bitcast_fusion.5
  495.1 2.8 dynamic-slice_bitcast_fusion.6
  497.8 84.2 %while.114 = (s32[]{:T(128)}, f32[128,2048]{1,0:T(8,128)S(1)}, bf16[18,16,16]{1,2,0:T(8,128)(2,1)S(1)}, bf16[18,128,128]{2,1,0:T(8,128)(2,1)}, s32[18]{0:T(128)S...) while((s32[]{:T(128)}, f32[128,2048]{1,0:T(8,128)S(1)}, ...), condition=%wide.region_26.26_spmd.clone, body=%wide.region_25.25_spmd.clone.sunk | while | flops 143654912 | bytes 6887093 | solution.py:61
  499.7 1.4 fusion.320
  504.4 1.4 fusion.320
  509.1 1.4 fusion.320
  513.8 1.4 fusion.320
  518.4 1.4 fusion.320
  523.1 1.4 fusion.320
  527.8 1.4 fusion.320
  541.8 1.4 fusion.320
  555.9 1.4 fusion.320
  569.9 1.4 fusion.320
  583.1 2.2 dynamic-slice_bitcast_fusion.5
  585.2 2.8 dynamic-slice_bitcast_fusion.6
  588.0 84.2 %while.114 = (s32[]{:T(128)}, f32[128,2048]{1,0:T(8,128)S(1)}, bf16[18,16,16]{1,2,0:T(8,128)(2,1)S(1)}, bf16[18,128,128]{2,1,0:T(8,128)(2,1)}, s32[18]{0:T(128)S...) while((s32[]{:T(128)}, f32[128,2048]{1,0:T(8,128)S(1)}, ...), condition=%wide.region_26.26_spmd.clone, body=%wide.region_25.25_spmd.clone.sunk | while | flops 143654912 | bytes 6887093 | solution.py:61
  589.9 1.4 fusion.320
  603.9 1.4 fusion.320
  617.9 1.4 fusion.320
  632.0 1.4 fusion.320
  646.0 1.4 fusion.320
  660.0 1.4 fusion.320
  673.3 3.8 fusion.232
  677.1 65.5 %all-reduce.1 = (f32[]{:T(128)}, f32[]{:T(128)}) all-reduce(f32[]{:T(128)} %get-tuple-element.594, f32[]{:T(128)} %get-tuple-element.593), channel_id=1, replica_groups=mesh['site'=4,'blk'=16,'charge'=2] {'blk','charge'}, use_global_device_ids=true, to_apply=%region_29.30 | all-reduce | flops 2 | bytes 16 | tf_op jit(solution)/shard_map/psum | solution.py:136
  743.9 3.3 multiply_reduce_fusion
  747.2 46.6 %conditional.7 = (bf16[1,2,18,128,128]{4,3,2,1,0:T(8,128)(2,1)}) conditional(s32[]{:T(128)} %convert_element_type.194, (bf16[2,18,128,128]{3,2,1,0:T(8,128)(2,1)S(1)}) %tuple.287, (bf16[2,2,4,128,128]{3,4,2,1,0:T(8,128)(2,1)S(1)}, bf16[2,18,18,4,4]{1,2,4,3,0:T(8,128)(2,1)S(1)}, bf16[2,18,128,128]{3,2,1,0:T(8,128)(2,1)S(1)}) %tuple.296), branch_computations={%region_18.19_spmd, %region_19.24_spmd} | conditional | flops 1553006592 | bytes 31303258 | solution.py:107
  749.0 21.7 %while.109 = (s32[]{:T(128)}, bf16[2,18,128,128]{2,3,1,0:T(8,128)(2,1)S(1)}, bf16[2,4,128,128]{2,3,1,0:T(8,128)(2,1)}, bf16[2,18,128,128]{3,2,1,0:T(8,128)(2,1)S(1)}, bf16[18,18,4,4]{0,1,3,2:T(8,128)(2,1)}, /*index=5*/s32[]{:T(128)}) while((s32[]{:T(128)}, bf16[2,18,128,128]{2,3,1,0:T(8,128)(2,1)S(1)}, bf16[2,4,128,128]{2,3,1,0:T(8,128)(2,1)}, ...), condition=%wide.region_21.21_spmd, body=%wide.region_20.20_spmd.sunk | while | flops 776503296 | bytes 12767997 | solution.py:42
  749.2 1.7 convert_bitcast_fusion.16
  751.0 7.2 fusion.328
  758.2 1.7 fusion.329
  760.0 1.7 convert_bitcast_fusion.16
  761.7 7.2 fusion.328
  768.9 1.7 fusion.329
  770.9 21.3 %while.110 = (s32[]{:T(128)}, bf16[2,18,128,128]{2,3,1,0:T(8,128)(2,1)S(1)}, bf16[2,4,128,128]{2,3,1,0:T(8,128)(2,1)}, bf16[2,18,128,128]{2,3,1,0:T(8,128)(2,1)S...) while((s32[]{:T(128)}, bf16[2,18,128,128]{2,3,1,0:T(8,128)(2,1)S(1)}, ...), condition=%wide.region_23.23_spmd, body=%wide.region_22.22_spmd.sunk | while | flops 776503296 | bytes 12726497 | solution.py:42
  770.9 1.7 convert_bitcast_fusion.17
  772.6 7.2 fusion.336
  779.8 1.7 fusion.337
  781.6 1.7 convert_bitcast_fusion.17
  783.3 7.2 fusion.336
  790.5 1.7 fusion.337
  792.3 1.4 copy.172
  793.9 63.2 %psum.23 = f32[]{:T(128)} all-reduce(f32[]{:T(128)} %multiply_reduce_fusion), channel_id=1, replica_groups=mesh['site'=4,'blk'=16,'charge'=2] {'blk','charge'}, use_global_device_ids=true, to_apply=%region_33.34 | all-reduce | flops 1 | bytes 8 | tf_op jit(solution)/shard_map/psum | solution.py:141
  857.8 3.3 fusion.234
  (248 shorter events, 111.6 us)
Async XLA Ops:
  1.9 0.5 copy-start.18
  19.1 7.0 copy-start.15
  19.1 7.3 copy-start.16
  19.1 7.6 copy-start.2
  19.1 304.2 %all-to-all-start = ((bf16[16,2,128,2048]{3,1,2,0:T(2,128)(2,1)}), bf16[16,2,128,2048]{3,1,2,0:T(2,128)(2,1)}, u32[]{:S(2)}, u32[]{:S(2)}) async-start(bf16[16,2,128,2048]{3,1,2,0:T(2,128)(2,1)} %stack.13), calls=%async_computation | async-start | bytes 33554432 | tf_op jit(solution)/shard_map/all_to_all | solution.py:14
  26.3 351.4 %copy-start.5 = (bf16[1,2,2,4,128,128]{4,5,3,2,1,0:T(8,128)(2,1)}, bf16[1,2,2,4,128,128]{4,5,3,2,1,0:T(8,128)(2,1)S(1)}, u32[]{:S(2)}) copy-start(bf16[1,2,2,4,128,128]{4,5,3,2,1,0:T(8,128)(2,1)S(1)} %copy.79) | copy-start | bytes 1572868
  26.7 351.1 %copy-start.7 = (bf16[1,2,18,18,4,4]{2,3,5,4,1,0:T(8,128)(2,1)}, bf16[1,2,18,18,4,4]{2,3,5,4,1,0:T(8,128)(2,1)S(1)}, u32[]{:S(2)}) copy-start(bf16[1,2,18,18,4,4]{2,3,5,4,1,0:T(8,128)(2,1)S(1)} %copy.80) | copy-start | bytes 62212
  26.7 2.9 copy-start.23
  26.7 11.3 %copy-start.25 = (u32[128]{0:T(128)S(1)}, u32[128]{0:T(128)}, u32[]{:S(2)}) copy-start(u32[128]{0:T(128)} %constant.180) | copy-start | bytes 1540
  26.7 292.0 %copy-start.22 = (s32[2]{0:T(128)S(1)}, s32[2]{0:T(128)}, u32[]{:S(2)}) copy-start(s32[2]{0:T(128)} %constant.168.clone) | copy-start | bytes 28
  28.3 290.5 %collective-permute-start = (bf16[2,18,128,128]{3,2,1,0:T(8,128)(2,1)}, bf16[2,18,128,128]{3,2,1,0:T(8,128)(2,1)S(1)}, u32[]{:S(2)}, u32[]{:S(2)}) collective-permute-start(bf16[2,18,128,128]{3,2,1,0:T(8,128)(2,1)} %get-tuple-element.585), channel_id=1, source_target_pairs={{0,32},{32,64},{64,96},{1,33},{33,65},{65,97},{2,34},{34,66},{66,9... | collective-permute-start | bytes 3538952 | tf_op jit(solution)/shard_map/ppermute | solution.py:21
  29.6 289.1 %collective-permute-start.3 = (s32[2]{0:T(128)S(1)}, s32[2]{0:T(128)S(1)}, u32[]{:S(2)}, u32[]{:S(2)}) collective-permute-start(s32[2]{0:T(128)S(1)} %bitcast.631), channel_id=1, source_target_pairs={{0,1},{1,0},{2,3},{3,2},{4,5},{5,4},{6,7},{7,6},{8,9},{9,8},{10,11... | collective-permute-start | bytes 32 | tf_op jit(solution)/shard_map/ppermute | solution.py:25
  318.8 2.8 copy-start.9
  321.6 53.3 %collective-permute-start.1 = (bf16[2,18,128,128]{3,2,1,0:T(8,128)(2,1)}, bf16[2,18,128,128]{3,2,1,0:T(8,128)(2,1)S(1)}, u32[]{:S(2)}, u32[]{:S(2)}) collective-permute-start(bf16[2,18,128,128]{3,2,1,0:T(8,128)(2,1)} %get-tuple-element.587), channel_id=1, source_target_pairs={{0,32},{32,64},{64,96},{1,33},{33,65},{65,97},{2,34},{34,66},{66,9... | collective-permute-start | bytes 3538952 | tf_op jit(solution)/shard_map/ppermute | solution.py:21
  373.4 102.9 %collective-permute-start.4 = (bf16[2,2,128,2048]{3,1,2,0:T(2,128)(2,1)}, bf16[2,2,128,2048]{3,1,2,0:T(2,128)(2,1)}, u32[]{:S(2)}, u32[]{:S(2)}) collective-permute-start(bf16[2,2,128,2048]{3,1,2,0:T(2,128)(2,1)} %convolution_convert_fusion.2), channel_id=1, source_target_pairs={{0,1},{1,0},{2,3},{3,2},{4,5},{5,4},{6,7},{7,6},{8,9},{9,8},{10,11... | collective-permute-start | bytes 6291464 | tf_op jit(solution)/shard_map/ppermute | solution.py:25
  374.9 2.8 copy-start.11
  377.8 2.7 copy-start
  377.8 2.7 copy-start.19
  377.8 95.3 %collective-permute-start.2 = (bf16[2,18,128,128]{3,2,1,0:T(8,128)(2,1)}, bf16[2,18,128,128]{3,2,1,0:T(8,128)(2,1)}, u32[]{:S(2)}, u32[]{:S(2)}) collective-permute-start(bf16[2,18,128,128]{3,2,1,0:T(8,128)(2,1)} %get-tuple-element.589), channel_id=1, source_target_pairs={{0,32},{32,64},{64,96},{1,33},{33,65},{65,97},{2,34},{34,66},{66,9... | collective-permute-start | bytes 3538952 | tf_op jit(solution)/shard_map/ppermute | solution.py:21
  380.5 92.6 %copy-start.4 = (bf16[2,18,128,128]{3,2,1,0:T(8,128)(2,1)S(1)}, bf16[2,18,128,128]{3,2,1,0:T(8,128)(2,1)}, u32[]{:S(2)}) copy-start(bf16[2,18,128,128]{3,2,1,0:T(8,128)(2,1)} %get-tuple-element.589) | copy-start | bytes 3538948
  380.5 92.6 %copy-start.10 = (bf16[2,18,128,128]{3,2,1,0:T(8,128)(2,1)S(1)}, bf16[2,18,128,128]{3,2,1,0:T(8,128)(2,1)}, u32[]{:S(2)}) copy-start(bf16[2,18,128,128]{3,2,1,0:T(8,128)(2,1)} %copy-done.9) | copy-start | bytes 3538948
  489.0 3.9 copy-start.24
  492.9 180.4 %copy-start.20 = (f32[2,128]{1,0:T(2,128)S(1)}, f32[2,128]{1,0:T(2,128)}, u32[]{:S(2)}) copy-start(f32[2,128]{1,0:T(2,128)} %get-tuple-element.727) | copy-start | bytes 3076
  492.9 180.4 %copy-start.21 = (f32[1,2]{1,0:T(1,128)S(1)}, f32[1,2]{1,0:T(1,128)}, u32[]{:S(2)}) copy-start(f32[1,2]{1,0:T(1,128)} %param.45) | copy-start | bytes 28
  673.3 70.6 %copy-start.1 = (bf16[1,2,128,2048]{3,2,1,0:T(8,128)(2,1)S(1)}, bf16[1,2,128,2048]{3,2,1,0:T(8,128)(2,1)}, u32[]{:S(2)}) copy-start(bf16[1,2,128,2048]{3,2,1,0:T(8,128)(2,1)} %param.39) | copy-start | bytes 3145732
  673.3 70.6 %copy-start.3 = (bf16[2,18,128,128]{3,2,1,0:T(8,128)(2,1)S(1)}, bf16[2,18,128,128]{3,2,1,0:T(8,128)(2,1)}, u32[]{:S(2)}) copy-start(bf16[2,18,128,128]{3,2,1,0:T(8,128)(2,1)} %get-tuple-element.726) | copy-start | bytes 3538948
  673.3 70.6 %copy-start.6 = (bf16[1,2,2,4,128,128]{4,5,3,2,1,0:T(8,128)(2,1)S(1)}, bf16[1,2,2,4,128,128]{4,5,3,2,1,0:T(8,128)(2,1)}, u32[]{:S(2)}) copy-start(bf16[1,2,2,4,128,128]{4,5,3,2,1,0:T(8,128)(2,1)} %copy-done.5) | copy-start | bytes 1572868
  673.3 70.7 %copy-start.8 = (bf16[1,2,18,18,4,4]{2,3,5,4,1,0:T(8,128)(2,1)S(1)}, bf16[1,2,18,18,4,4]{2,3,5,4,1,0:T(8,128)(2,1)}, u32[]{:S(2)}) copy-start(bf16[1,2,18,18,4,4]{2,3,5,4,1,0:T(8,128)(2,1)} %copy-done.7) | copy-start | bytes 62212
  749.2 1.7 copy-start.17
  751.0 7.2 copy-start.14
  759.9 1.7 copy-start.17
  761.7 7.2 copy-start.14
  772.6 7.2 copy-start.12
  783.3 7.2 copy-start.12
